TPU v7x, 32 devices: a whole 2x2x4 slice. The times are simulated.
32 devices in a mesh: dp: 8 (over z, x), sp: 4 (over y, core).
Axes of the slice: x: 2, y: 2, z: 4, core: 2. Of those that a mesh axis runs over, the one named last changes fastest.
Arguments:
- hidden_in: bfloat16 [8, 1024, 512], P('dp', 'sp'), may hold values from -6 to 6
- cotangent: float32 [8, 1024, 512], P('dp', 'sp'), may hold values from -6 to 6
- lengths: int32 [8], P('dp'), may hold values from 256 to 1024, as said below
- master: float32 [6301696], P(('dp', 'sp'))
- moment_one: float32 [6301696], P(('dp', 'sp'))
- moment_two: float32 [6301696], P(('dp', 'sp'))
Outputs:
- output: float32 [8, 1024, 512], P('dp', 'sp')
- input_grad: float32 [8, 1024, 512], P('dp', 'sp')
- new_master: float32 [6301696], P(('dp', 'sp'))
- new_moment_one: float32 [6301696], P(('dp', 'sp'))
- new_moment_two: float32 [6301696], P(('dp', 'sp'))
- new_weights: bfloat16 [6301696], P(('dp', 'sp'))
- grad_norm: float32 [], replicated
- gains_grad: float32 [2, 2, 512], replicated
Inputs may be any that keep to these rules, and one draw needn't show every extreme that they name: `lengths`: in every draw one sequence has all 1024 tokens real and another only 256.
All inputs are finite; a program needn't handle non-finite values.
Results may differ from a plain program's by a relative error of at most 0.017.
Values may be sent and summed in bfloat16 or wider, within the bound.
A program may use at most 192 MiB of HBM per device.

v0:
```python
import jax
import jax.numpy as jnp
from jax import lax
from jax.sharding import PartitionSpec as P

D = 512
HEADS = 8
HEAD_DIM = 64
FF = 1368
SEQ = 1024
BLOCK = 512
STEP = 5
NORM_EPS = 1e-06
ADAM_EPS = 1e-08
LEARN_RATE = 0.02
DECAY_RATE = 0.01


def shortened(array):

    def short(part):
        return part.astype(jnp.bfloat16) if part.dtype == jnp.float32 else part

    return jax.tree.map(short, array)


def layer_pieces(flat_weights, layer_index):
    shapes = [(D, 3 * D), (D, D), (D, 2 * FF), (FF, D), (2, D)]
    offset = layer_index * (4 * D * D + 3 * D * FF + 2 * D)
    pieces = []
    for dims_pair in shapes:
        length_now = dims_pair[0] * dims_pair[1]
        pieces.append(flat_weights[offset : offset + length_now].reshape(dims_pair))
        offset = offset + length_now
    return pieces


def rope_tables(positions):
    half_dim = HEAD_DIM // 2
    frequency = jnp.exp(
        -jnp.log(10000.0) * jnp.arange(half_dim).astype(jnp.float32) * 2.0 / HEAD_DIM
    )
    angles = positions.astype(jnp.float32)[:, None] * frequency[None, :]
    return (jnp.cos(angles), jnp.sin(angles))


def rotate(values, cosine_table, sine_table):
    half_dim = values.shape[-1] // 2
    first_half = values[..., :half_dim]
    second_half = values[..., half_dim:]
    cos_rows = cosine_table[:, None, :]
    sin_rows = sine_table[:, None, :]
    return jnp.concatenate(
        [
            first_half * cos_rows - second_half * sin_rows,
            second_half * cos_rows + first_half * sin_rows,
        ],
        axis=-1,
    )


def unrotate(values, cosine_table, sine_table):
    half_dim = values.shape[-1] // 2
    first_half = values[..., :half_dim]
    second_half = values[..., half_dim:]
    cos_rows = cosine_table[:, None, :]
    sin_rows = sine_table[:, None, :]
    return jnp.concatenate(
        [
            first_half * cos_rows + second_half * sin_rows,
            second_half * cos_rows - first_half * sin_rows,
        ],
        axis=-1,
    )


def norm_forward(stream, gain):
    factor = lax.rsqrt(jnp.mean(stream * stream, axis=-1, keepdims=True) + NORM_EPS)
    return (stream * factor * gain, factor)


def norm_backward(upstream, stream, factor, gain):
    scaled = upstream * gain
    gain_grad = jnp.sum(upstream * stream * factor, axis=(0, 1))
    stream_grad = factor * scaled - stream * factor**3 * jnp.mean(
        scaled * stream, axis=-1, keepdims=True
    )
    return (stream_grad, gain_grad)


def block_logits(query_block, key_rows, offset, length_now):
    raw_scores = jnp.einsum(
        "qhd,khd->hqk", query_block, key_rows, preferred_element_type=jnp.float32
    )
    row_place = offset + jnp.arange(query_block.shape[0])[:, None]
    col_place = jnp.arange(key_rows.shape[0])[None, :]
    allowed = (col_place <= row_place) & (col_place < length_now)
    return jnp.where(allowed[None], raw_scores * HEAD_DIM ** (-0.5), -1000000000.0)


def attend_forward(packed_in):
    sequence, length_now = packed_in
    query_rows = sequence[:, 0]
    key_rows = sequence[:, 1]
    value_rows = sequence[:, 2]
    context_parts = []
    logsum_parts = []
    for offset in range(0, SEQ, BLOCK):
        logits = block_logits(query_rows[offset : offset + BLOCK], key_rows, offset, length_now)
        logsum = jax.nn.logsumexp(logits, axis=-1)
        weights_soft = jnp.exp(logits - logsum[..., None]).astype(jnp.bfloat16)
        context_parts.append(
            jnp.einsum("hqk,khd->qhd", weights_soft, value_rows, preferred_element_type=jnp.float32)
        )
        logsum_parts.append(logsum)
    return (jnp.concatenate(context_parts, 0), jnp.concatenate(logsum_parts, 1))


def attend_backward(packed_in):
    sequence, grad_context, logsum, length_now = packed_in
    query_rows = sequence[:, 0]
    key_rows = sequence[:, 1]
    value_rows = sequence[:, 2]
    grad_rows = grad_context.reshape(query_rows.shape)
    key_grad = jnp.zeros(key_rows.shape, jnp.float32)
    value_grad = jnp.zeros(value_rows.shape, jnp.float32)
    query_parts = []
    for offset in range(0, SEQ, BLOCK):
        query_block = query_rows[offset : offset + BLOCK]
        grad_block = grad_rows[offset : offset + BLOCK]
        logits = block_logits(query_block, key_rows, offset, length_now)
        weights_soft = jnp.exp(logits - logsum[:, offset : offset + BLOCK, None])
        value_grad = value_grad + jnp.einsum(
            "hqk,qhd->khd",
            weights_soft.astype(jnp.bfloat16),
            grad_block,
            preferred_element_type=jnp.float32,
        )
        weight_grad = jnp.einsum(
            "qhd,khd->hqk", grad_block, value_rows, preferred_element_type=jnp.float32
        )
        centered = weight_grad - jnp.sum(weights_soft * weight_grad, axis=-1, keepdims=True)
        score_grad = (weights_soft * centered * HEAD_DIM ** (-0.5)).astype(jnp.bfloat16)
        query_parts.append(
            jnp.einsum("hqk,khd->qhd", score_grad, key_rows, preferred_element_type=jnp.float32)
        )
        key_grad = key_grad + jnp.einsum(
            "hqk,qhd->khd", score_grad, query_block, preferred_element_type=jnp.float32
        )
    query_grad = jnp.concatenate(query_parts, 0)
    return jnp.stack([query_grad, key_grad, value_grad], axis=1).astype(jnp.bfloat16)


def attention_forward(stream, weight_qkv, weight_out, cosine_table, sine_table, lengths):
    seq_count, row_count, feature_count = stream.shape
    groups = lax.axis_size("sp")
    head_local = HEADS // groups
    inputs_low = stream.astype(jnp.bfloat16).reshape(-1, feature_count)
    projected = jnp.dot(inputs_low, weight_qkv, preferred_element_type=jnp.float32).reshape(
        seq_count, row_count, 3, HEADS, HEAD_DIM
    )
    rotated = jnp.stack(
        [
            rotate(projected[:, :, 0], cosine_table, sine_table),
            rotate(projected[:, :, 1], cosine_table, sine_table),
            projected[:, :, 2],
        ],
        axis=2,
    )
    outgoing = rotated.astype(jnp.bfloat16).reshape(
        seq_count, row_count, 3, groups, head_local * HEAD_DIM
    )
    by_heads = lax.all_to_all(outgoing, "sp", split_axis=3, concat_axis=1, tiled=True)
    by_heads = by_heads.reshape(seq_count, row_count * groups, 3, head_local, HEAD_DIM)
    context, logsum = lax.map(attend_forward, (by_heads, lengths))
    context_low = context.astype(jnp.bfloat16).reshape(
        seq_count, row_count * groups, 1, head_local * HEAD_DIM
    )
    by_tokens = lax.all_to_all(context_low, "sp", split_axis=1, concat_axis=2, tiled=True)
    context_rows = by_tokens.reshape(-1, feature_count)
    branch = jnp.dot(context_rows, weight_out, preferred_element_type=jnp.float32).reshape(
        seq_count, row_count, feature_count
    )
    return (branch, (inputs_low, context_rows, by_heads, logsum))


def attention_backward(upstream, saved, weight_qkv, weight_out, cosine_table, sine_table, lengths):
    inputs_low, context_rows, by_heads, logsum = saved
    seq_count, row_count, feature_count = upstream.shape
    groups = lax.axis_size("sp")
    head_local = HEADS // groups
    upstream_low = upstream.astype(jnp.bfloat16).reshape(-1, feature_count)
    out_grad = jnp.einsum(
        "nd,ne->de", context_rows, upstream_low, preferred_element_type=jnp.float32
    )
    context_grad = jnp.dot(upstream_low, weight_out.T, preferred_element_type=jnp.float32).astype(
        jnp.bfloat16
    )
    context_grad = context_grad.reshape(seq_count, row_count, groups, head_local * HEAD_DIM)
    grad_heads = lax.all_to_all(context_grad, "sp", split_axis=2, concat_axis=1, tiled=True)
    head_grads = lax.map(attend_backward, (by_heads, grad_heads, logsum, lengths))
    outgoing = head_grads.reshape(seq_count, row_count * groups, 3, 1, head_local * HEAD_DIM)
    token_grads = lax.all_to_all(
        shortened(outgoing), "sp", split_axis=1, concat_axis=3, tiled=True
    ).astype(outgoing.dtype)
    token_grads = token_grads.reshape(seq_count, row_count, 3, HEADS, HEAD_DIM).astype(jnp.float32)
    lin_grad = jnp.stack(
        [
            unrotate(token_grads[:, :, 0], cosine_table, sine_table),
            unrotate(token_grads[:, :, 1], cosine_table, sine_table),
            token_grads[:, :, 2],
        ],
        axis=2,
    )
    lin_grad = lin_grad.astype(jnp.bfloat16).reshape(-1, 3 * feature_count)
    qkv_grad = jnp.einsum("nd,ne->de", inputs_low, lin_grad, preferred_element_type=jnp.float32)
    input_grad = jnp.dot(lin_grad, weight_qkv.T, preferred_element_type=jnp.float32).reshape(
        seq_count, row_count, feature_count
    )
    return (input_grad, qkv_grad, out_grad)


def ffn_forward(stream, weight_gu, weight_down):
    seq_count, row_count, feature_count = stream.shape
    inputs_low = stream.astype(jnp.bfloat16).reshape(-1, feature_count)
    both_parts = jnp.dot(inputs_low, weight_gu, preferred_element_type=jnp.float32)
    units = (jax.nn.silu(both_parts[:, :FF]) * both_parts[:, FF:]).astype(jnp.bfloat16)
    branch = jnp.dot(units, weight_down, preferred_element_type=jnp.float32).reshape(
        seq_count, row_count, feature_count
    )
    return (branch, (inputs_low, both_parts, units))


def ffn_backward(upstream, saved, weight_gu, weight_down):
    inputs_low, both_parts, units = saved
    seq_count, row_count, feature_count = upstream.shape
    upstream_low = upstream.astype(jnp.bfloat16).reshape(-1, feature_count)
    down_grad = jnp.einsum("nf,nd->fd", units, upstream_low, preferred_element_type=jnp.float32)
    units_grad = jnp.dot(upstream_low, weight_down.T, preferred_element_type=jnp.float32)
    gate_part = both_parts[:, :FF]
    up_part = both_parts[:, FF:]
    sigmoid_part = jax.nn.sigmoid(gate_part)
    gate_grad = units_grad * up_part * sigmoid_part * (1.0 + gate_part * (1.0 - sigmoid_part))
    up_grad = units_grad * gate_part * sigmoid_part
    both_grad = jnp.concatenate([gate_grad, up_grad], axis=1).astype(jnp.bfloat16)
    gu_grad = jnp.einsum("nd,nf->df", inputs_low, both_grad, preferred_element_type=jnp.float32)
    input_grad = jnp.dot(both_grad, weight_gu.T, preferred_element_type=jnp.float32).reshape(
        seq_count, row_count, feature_count
    )
    return (input_grad, gu_grad, down_grad)


def shards(hidden_in, cotangent, lengths, master, moment_one, moment_two):
    shard_low = master.astype(jnp.bfloat16)
    flat_weights = lax.all_gather(shard_low, ("dp", "sp"), axis=0, tiled=True)
    seq_count, row_count, feature_count = hidden_in.shape
    positions = lax.axis_index("sp") * row_count + jnp.arange(row_count)
    cosine_table, sine_table = rope_tables(positions)
    first_weights = layer_pieces(flat_weights, 0)
    second_weights = layer_pieces(flat_weights, 1)
    gains_first = first_weights[4].astype(jnp.float32)
    gains_second = second_weights[4].astype(jnp.float32)
    stream_zero = hidden_in.astype(jnp.float32)
    attn_zero, attn_zero_saved = attention_forward(
        stream_zero, first_weights[0], first_weights[1], cosine_table, sine_table, lengths
    )
    resid_one = stream_zero + attn_zero
    stream_one, factor_one = norm_forward(resid_one, gains_first[0])
    ffn_zero, ffn_zero_saved = ffn_forward(stream_one, first_weights[2], first_weights[3])
    resid_two = stream_one + ffn_zero
    stream_two, factor_two = norm_forward(resid_two, gains_first[1])
    normed_three, factor_three = norm_forward(stream_two, gains_second[0])
    attn_one, attn_one_saved = attention_forward(
        normed_three, second_weights[0], second_weights[1], cosine_table, sine_table, lengths
    )
    stream_three = stream_two + attn_one
    normed_four, factor_four = norm_forward(stream_three, gains_second[1])
    ffn_one, ffn_one_saved = ffn_forward(normed_four, second_weights[2], second_weights[3])
    output = stream_three + ffn_one
    keep = (positions[None, :] < lengths[:, None]).astype(jnp.float32)
    upstream = cotangent * keep[:, :, None]
    ffn_in_grad, gu_grad_one, down_grad_one = ffn_backward(
        upstream, ffn_one_saved, second_weights[2], second_weights[3]
    )
    norm_part, gain_grad_four = norm_backward(
        ffn_in_grad, stream_three, factor_four, gains_second[1]
    )
    three_grad = upstream + norm_part
    attn_in_grad, qkv_grad_one, out_grad_one = attention_backward(
        three_grad,
        attn_one_saved,
        second_weights[0],
        second_weights[1],
        cosine_table,
        sine_table,
        lengths,
    )
    norm_part, gain_grad_three = norm_backward(
        attn_in_grad, stream_two, factor_three, gains_second[0]
    )
    two_grad = three_grad + norm_part
    resid_two_grad, gain_grad_two = norm_backward(two_grad, resid_two, factor_two, gains_first[1])
    ffn_in_grad, gu_grad_zero, down_grad_zero = ffn_backward(
        resid_two_grad, ffn_zero_saved, first_weights[2], first_weights[3]
    )
    one_grad = resid_two_grad + ffn_in_grad
    resid_one_grad, gain_grad_one = norm_backward(one_grad, resid_one, factor_one, gains_first[0])
    attn_in_grad, qkv_grad_zero, out_grad_zero = attention_backward(
        resid_one_grad,
        attn_zero_saved,
        first_weights[0],
        first_weights[1],
        cosine_table,
        sine_table,
        lengths,
    )
    input_grad = resid_one_grad + attn_in_grad
    gains_first_grad = jnp.stack([gain_grad_one, gain_grad_two])
    gains_second_grad = jnp.stack([gain_grad_three, gain_grad_four])
    grad_flat = jnp.concatenate(
        [
            qkv_grad_zero.reshape(-1),
            out_grad_zero.reshape(-1),
            gu_grad_zero.reshape(-1),
            down_grad_zero.reshape(-1),
            gains_first_grad.reshape(-1),
            qkv_grad_one.reshape(-1),
            out_grad_one.reshape(-1),
            gu_grad_one.reshape(-1),
            down_grad_one.reshape(-1),
            gains_second_grad.reshape(-1),
        ]
    )
    grad_grid = grad_flat.reshape(lax.axis_size("dp"), lax.axis_size("sp"), -1)
    partial_sum = lax.psum_scatter(
        grad_grid.astype(jnp.bfloat16), "sp", scatter_dimension=1, tiled=True
    ).astype(jnp.float32)
    grad_shard = lax.psum_scatter(partial_sum, "dp", scatter_dimension=0, tiled=True).reshape(-1)
    gains_local = jnp.stack([gains_first_grad, gains_second_grad])
    squares, gains_grad = lax.psum((jnp.sum(grad_shard * grad_shard), gains_local), ("dp", "sp"))
    grad_norm = jnp.sqrt(squares)
    clipped = grad_shard * jnp.minimum(1.0, 1.0 / grad_norm)
    new_one = 0.5 * moment_one + 0.5 * clipped
    new_two = 0.5 * moment_two + 0.5 * clipped * clipped
    correction = 1.0 - 0.5**STEP
    new_master = master * (1.0 - LEARN_RATE * DECAY_RATE) - LEARN_RATE * (new_one / correction) / (
        jnp.sqrt(new_two / correction) + ADAM_EPS
    )
    return (
        output,
        input_grad,
        new_master,
        new_one,
        new_two,
        new_master.astype(jnp.bfloat16),
        grad_norm,
        gains_grad,
    )


def solution(mesh):
    in_specs = (
        P("dp", "sp", None),
        P("dp", "sp", None),
        P("dp"),
        P(("dp", "sp")),
        P(("dp", "sp")),
        P(("dp", "sp")),
    )
    out_specs = (
        P("dp", "sp", None),
        P("dp", "sp", None),
        P(("dp", "sp")),
        P(("dp", "sp")),
        P(("dp", "sp")),
        P(("dp", "sp")),
        P(),
        P(),
    )
    return jax.shard_map(shards, mesh=mesh, in_specs=in_specs, out_specs=out_specs, check_vma=False)
```

profile of v0, /device:TPU:12, one launch (start us, length us, event | category | flops | bytes accessed | tf_op | source)
XLA Modules:
  0.0 1094.7 jit_solution(13723838610632103288)
XLA Ops:
  8.4 4.7 broadcast.325
  13.1 7.3 dynamic-update-slice
  22.6 230.5 %all-reduce.7.cloned.1.call-done = bf16[6301696]{0:T(1024)(128)(2,1)} async-done(((bf16[6301696]{0:T(1024)(128)(2,1)}), bf16[6301696]{0:T(1024)(128)(2,1)}) %all-reduce.7.cloned.1.call-update) | async-done | bytes 12603408
  265.3 4.7 all-to-all-start
  286.4 5.8 reshape.1048
  293.6 13.9 %slice.340 = bf16[1368,512]{1,0:T(8,128)(2,1)} reshape(bf16[700416]{0:T(1024)(128)(2,1)} %get-tuple-element.90) | data formatting | bytes 2801664 | tf_op jit(solution)/shard_map/slice | solution.py:33
  337.8 14.3 %all_to_all.108 = bf16[1,256,3,4,128]{1,4,2,0,3:T(8,128)(2,1)S(1)} all-to-all(bf16[1,256,3,4,128]{1,4,2,0,3:T(8,128)(2,1)S(1)} %pad_maximum_fusion.9), channel_id=1, replica_groups=mesh['dp'=8,'sp'=4] {'sp'}, dimensions={3} | all-to-all | bytes 1572864 | tf_op jit(solution)/shard_map/all_to_all | solution.py:173
  373.9 6.1 all-to-all-start.3
  381.3 7.2 reshape.1055
  407.6 7.6 all_to_all.109
  427.5 12.8 %fusion.22 = f32[2,64,1024]{2,1,0:T(8,128)} fusion(f32[2,512,1024]{2,1,0:T(8,128)} %fusion.143, bf16[1024,3,2,64]{0,3,2,1:T(8,128)(2,1)} %squeeze.98, f32[2,512,1024]{2,1,0:T(8,128)} %get-tuple-element.167, f32[2,512]{1,0:T(2,128)S(1)} %log_add_fusion.1, pred[512,1024]{1,0:T(8,128)(4,1)S(1)} %copy-done.23), kind=kOutput, calls=%fused_computation.39 | convolution fusion | flops 145754112 | bytes 18489344 | tf_op jit(solution)/shard_map/while/body/eval_jaxpr/hqk,qhd->khd/dot_general | solution.py:147
  440.3 12.5 %fusion.91 = bf16[512,2,64]{0,2,1:T(8,128)(2,1)} fusion(f32[2,512,1024]{2,1,0:T(8,128)} %fusion.143, bf16[1024,3,2,64]{0,3,2,1:T(8,128)(2,1)} %squeeze.98, f32[2,512,1024]{2,1,0:T(8,128)} %get-tuple-element.167, f32[2,512]{1,0:T(2,128)S(1)} %log_add_fusion.1, pred[512,1024]{1,0:T(8,128)(4,1)S(1)} %copy-done.23), kind=kOutput, calls=%fused_computation.109 | convolution fusion | flops 145819648 | bytes 18227200 | tf_op jit(solution)/shard_map/while/body/eval_jaxpr/hqk,khd->qhd/dot_general | solution.py:145
  465.3 12.2 %fusion.94 = bf16[512,2,64]{0,2,1:T(8,128)(2,1)} fusion(f32[2,512,1024]{2,1,0:T(8,128)} %fusion.142, bf16[1024,3,2,64]{0,3,2,1:T(8,128)(2,1)} %squeeze.98, f32[2,512,1024]{2,1,0:T(8,128)} %copy-done.31, f32[2,512]{1,0:T(2,128)S(1)} %log_add_fusion, pred[512,1024]{1,0:T(8,128)(4,1)S(1)} %copy-done.22), kind=kOutput, calls=%fused_computation.110 | convolution fusion | flops 145819648 | bytes 18227200 | tf_op jit(solution)/shard_map/while/body/eval_jaxpr/hqk,khd->qhd/dot_general | solution.py:145
  477.5 12.6 %fusion.73 = bf16[2,64,1024]{2,1,0:T(8,128)(2,1)} fusion(f32[2,64,1024]{2,1,0:T(8,128)} %fusion.22, f32[2,512,1024]{2,1,0:T(8,128)} %fusion.142, bf16[1024,3,2,64]{0,3,2,1:T(8,128)(2,1)} %squeeze.98, f32[2,512,1024]{2,1,0:T(8,128)} %copy-done.31, f32[2,512]{1,0:T(2,128)S(1)} %log_add_fusion, pred[512,1024]{1,0:T(8,128)(4,1)S(1)} %copy-done.22), kind=kOutput, calls=%fused_computation.95 | convolution fusion | flops 146016256 | bytes 18751488 | tf_op jit(solution)/shard_map/while/body/eval_jaxpr/hqk,qhd->khd/dot_general | solution.py:147
  499.8 6.3 all-to-all-start.5
  512.2 4.5 copy.134
  516.7 6.4 reshape.1072
  563.0 13.1 %fusion.34 = f32[2,64,1024]{2,1,0:T(8,128)} fusion(f32[2,512,1024]{2,1,0:T(8,128)} %fusion.139, bf16[1024,3,2,64]{0,3,2,1:T(8,128)(2,1)} %copy-done.41, f32[2,512,1024]{2,1,0:T(8,128)} %copy-done.30, f32[2,512]{1,0:T(2,128)S(1)} %log_add_fusion.3, pred[512,1024]{1,0:T(8,128)(4,1)} %get-tuple-element.154), kind=kOutput, calls=%fused_computation.43 | convolution fusion | flops 145754112 | bytes 18489344 | tf_op jit(solution)/shard_map/while/body/eval_jaxpr/hqk,qhd->khd/dot_general | solution.py:147
  576.1 12.8 %fusion.97 = bf16[512,2,64]{0,2,1:T(8,128)(2,1)} fusion(f32[2,512,1024]{2,1,0:T(8,128)} %fusion.139, bf16[1024,3,2,64]{0,3,2,1:T(8,128)(2,1)} %copy-done.41, f32[2,512,1024]{2,1,0:T(8,128)} %copy-done.30, f32[2,512]{1,0:T(2,128)S(1)} %log_add_fusion.3, pred[512,1024]{1,0:T(8,128)(4,1)} %get-tuple-element.154), kind=kOutput, calls=%fused_computation.111 | convolution fusion | flops 145819648 | bytes 18227200 | tf_op jit(solution)/shard_map/while/body/eval_jaxpr/hqk,khd->qhd/dot_general | solution.py:145
  595.0 12.3 %fusion.100 = bf16[512,2,64]{0,2,1:T(8,128)(2,1)} fusion(f32[2,512,1024]{2,1,0:T(8,128)} %fusion.138, bf16[1024,3,2,64]{0,3,2,1:T(8,128)(2,1)} %copy-done.41, f32[2,512,1024]{2,1,0:T(8,128)} %copy-done.28, f32[2,512]{1,0:T(2,128)S(1)} %log_add_fusion.2, pred[512,1024]{1,0:T(8,128)(4,1)S(1)} %copy-done.22), kind=kOutput, calls=%fused_computation.112 | convolution fusion | flops 145819648 | bytes 18227200 | tf_op jit(solution)/shard_map/while/body/eval_jaxpr/hqk,khd->qhd/dot_general | solution.py:145
  607.3 12.0 %fusion.76 = bf16[2,64,1024]{2,1,0:T(8,128)(2,1)S(1)} fusion(f32[2,64,1024]{2,1,0:T(8,128)} %fusion.34, f32[2,512,1024]{2,1,0:T(8,128)} %fusion.138, bf16[1024,3,2,64]{0,3,2,1:T(8,128)(2,1)} %copy-done.41, f32[2,512,1024]{2,1,0:T(8,128)} %copy-done.28, f32[2,512]{1,0:T(2,128)S(1)} %log_add_fusion.2, pred[512,1024]{1,0:T(8,128)(4,1)S(1)} %copy-done.22), kind=kOutput, calls=%fused_computation.96 | convolution fusion | flops 146016256 | bytes 18751488 | tf_op jit(solution)/shard_map/while/body/eval_jaxpr/hqk,qhd->khd/dot_general | solution.py:147
  625.6 4.6 all-to-all-start.7
  631.5 5.0 copy.133
  636.5 6.5 reshape.1067
  653.9 4.4 reshape.1065
  672.0 23.6 %convert_element_type.303 = bf16[8,4,196928]{2,1,0:T(4,128)(2,1)} reshape(bf16[6301696]{0:T(1024)(128)(2,1)} %constant_dynamic-update-slice_fusion) | data formatting | bytes 25206784 | tf_op jit(solution)/shard_map/convert_element_type | solution.py:336
  695.6 11.5 %copy.135 = bf16[8,4,196928]{2,0,1:T(8,128)(2,1)} copy(bf16[8,4,196928]{2,1,0:T(4,128)(2,1)} %convert_element_type.303) | data formatting | bytes 25206784 | tf_op jit(solution)/shard_map/convert_element_type | solution.py:336
  707.2 98.9 %reduce-scatter.4.cloned.1.call-done = bf16[8,1,196928]{2,0,1:T(8,128)(2,1)} async-done(((bf16[8,4,196928]{2,0,1:T(8,128)(2,1)}), bf16[8,1,196928]{2,0,1:T(8,128)(2,1)}) %reduce-scatter.4.cloned.1.call-update) | async-done | bytes 3150864
  806.1 6.9 copy.136
  817.3 208.4 %all-reduce.9.cloned.1.call-done = f32[8,1,196928]{2,1,0:T(1,128)} async-done(((f32[8,1,196928]{2,1,0:T(1,128)}), f32[8,1,196928]{2,1,0:T(1,128)}) %all-reduce.9.cloned.1.call-update) | async-done | bytes 6301712
  1031.0 42.5 %all-reduce.3 = (f32[]{:T(128)}, f32[2,2,512]{2,1,0:T(2,128)}) all-reduce(f32[]{:T(128)} %multiply_reduce_fusion.5, f32[2,2,512]{2,1,0:T(2,128)S(1)} %pad_maximum_fusion.20), channel_id=1, replica_groups=mesh['dp'=8,'sp'=4] {'dp','sp'}, use_global_device_ids=true, to_apply=%region_27.28 | all-reduce | flops 2049 | bytes 16392 | tf_op jit(solution)/shard_map/psum | solution.py:340
  1074.3 9.0 multiply_reduce_fusion.4
  (309 shorter events, 236.0 us)
Async XLA Ops:
  7.2 245.9 %all-reduce.7.cloned.1.call-start = ((), (), s32[]{:S(2)}) async-start(), calls=%async_computation.9 | async-start | bytes 25206784
  22.6 340.1 %copy-start.21 = (pred[512,1024]{1,0:T(8,128)(4,1)}, pred[512,1024]{1,0:T(8,128)(4,1)S(1)}, u32[]{:S(2)}) copy-start(pred[512,1024]{1,0:T(8,128)(4,1)S(1)} %get-tuple-element.155) | copy-start | bytes 1572868
  256.9 5.1 copy-start.38
  260.2 3.9 copy-start
  265.3 42.9 %all-to-all-start = ((bf16[1,256,3,4,128]{1,4,2,0,3:T(8,128)(2,1)}), bf16[1,256,3,4,128]{1,4,2,0,3:T(8,128)(2,1)}, u32[]{:S(2)}, u32[]{:S(2)}) async-start(bf16[1,256,3,4,128]{1,4,2,0,3:T(8,128)(2,1)} %pad_maximum_fusion.8), calls=%async_computation | async-start | bytes 1572864 | tf_op jit(solution)/shard_map/all_to_all | solution.py:173
  293.6 37.0 %copy-start.26 = (bf16[512,512]{1,0:T(8,128)(2,1)}, bf16[512,512]{1,0:T(8,128)(2,1)S(1)}, u32[]{:S(2)}) copy-start(bf16[512,512]{1,0:T(8,128)(2,1)S(1)} %slice.333) | copy-start | bytes 1572868
  310.5 6.1 copy-start.41
  317.9 12.7 %copy-start.39 = (bf16[1,256,512]{2,1,0:T(8,128)(2,1)S(1)}, bf16[1,256,512]{2,1,0:T(8,128)(2,1)}, u32[]{:S(2)}) copy-start(bf16[1,256,512]{2,1,0:T(8,128)(2,1)} %param.6) | copy-start | bytes 786436
  322.3 7.8 all-to-all-start.1
  330.6 4.2 copy-start.36
  358.3 4.5 copy-start.31
  373.9 18.2 %all-to-all-start.3 = ((bf16[4,2,16384]{2,1,0:T(2,128)(2,1)}), bf16[4,2,16384]{2,1,0:T(2,128)(2,1)}, u32[]{:S(2)}, u32[]{:S(2)}) async-start(bf16[4,2,16384]{2,1,0:T(2,128)(2,1)} %reshape.1086), calls=%async_computation.3 | async-start | bytes 524288 | tf_op jit(solution)/shard_map/all_to_all | solution.py:179
  381.3 14.5 %copy-start.24 = (bf16[512,512]{1,0:T(8,128)(2,1)}, bf16[512,512]{1,0:T(8,128)(2,1)S(1)}, u32[]{:S(2)}) copy-start(bf16[512,512]{1,0:T(8,128)(2,1)S(1)} %slice.359) | copy-start | bytes 1572868
  395.8 4.7 copy-start.15
  395.8 4.7 copy-start.43
  419.3 4.4 copy-start.52
  452.7 7.2 copy-start.22
  499.8 27.0 %all-to-all-start.5 = ((bf16[1,1024,3,1,128]{4,2,3,0,1:T(4,128)(2,1)}), bf16[1,1024,3,1,128]{4,2,3,0,1:T(4,128)(2,1)}, u32[]{:S(2)}, u32[]{:S(2)}) async-start(bf16[1,1024,3,1,128]{4,2,3,0,1:T(4,128)(2,1)} %pad_maximum_fusion.2), calls=%async_computation.5 | async-start | bytes 2097152 | tf_op jit(solution)/shard_map/all_to_all | solution.py:203
  540.2 90.0 %copy-start.8 = (f32[1,256,512]{2,1,0:T(8,128)}, f32[1,256,512]{2,1,0:T(8,128)S(1)}, u32[]{:S(2)}) copy-start(f32[1,256,512]{2,1,0:T(8,128)S(1)} %multiply_subtract_fusion) | copy-start | bytes 1572868
  544.7 9.8 all-to-all-start.6
  548.9 3.9 copy-start.46
  619.2 10.9 copy-start.37
  625.6 23.0 %all-to-all-start.7 = ((bf16[1,1024,3,1,128]{4,2,3,0,1:T(4,128)(2,1)}), bf16[1,1024,3,1,128]{4,2,3,0,1:T(4,128)(2,1)}, u32[]{:S(2)}, u32[]{:S(2)}) async-start(bf16[1,1024,3,1,128]{4,2,3,0,1:T(4,128)(2,1)} %pad_maximum_fusion.3), calls=%async_computation.7 | async-start | bytes 2097152 | tf_op jit(solution)/shard_map/all_to_all | solution.py:203
  630.2 175.9 %reduce-scatter.4.cloned.1.call-start = ((), (), s32[]{:S(2)}) async-start(), calls=%async_computation.11 | async-start | bytes 15759360
  636.4 6.5 copy-start.16
  636.4 8.4 copy-start.35
  653.9 9.1 copy-start.7
  658.4 6.4 copy-start.20
  707.2 318.5 %all-reduce.9.cloned.1.call-start = ((), (), s32[]{:S(2)}) async-start(), calls=%async_computation.10 | async-start | bytes 12607488
  813.0 216.5 %copy-start.1 = (bf16[512,1536]{1,0:T(8,128)(2,1)S(1)}, bf16[512,1536]{1,0:T(8,128)(2,1)}, u32[]{:S(2)}) copy-start(bf16[512,1536]{1,0:T(8,128)(2,1)} %copy-done) | copy-start | bytes 4718596
  813.0 216.5 %copy-start.9 = (f32[1,256,512]{2,1,0:T(8,128)S(1)}, f32[1,256,512]{2,1,0:T(8,128)}, u32[]{:S(2)}) copy-start(f32[1,256,512]{2,1,0:T(8,128)} %copy-done.8) | copy-start | bytes 1572868
  813.0 216.5 %copy-start.11 = (bf16[1,256,3,8,64]{1,4,3,2,0:T(8,128)(2,1)S(1)}, bf16[1,256,3,8,64]{1,4,3,2,0:T(8,128)(2,1)}, u32[]{:S(2)}) copy-start(bf16[1,256,3,8,64]{1,4,3,2,0:T(8,128)(2,1)} %copy-done.10) | copy-start | bytes 2359300
  (31 other events, 73.9 us)
Sparse Core Ops, SparseCore 0:
  20.5 232.5 all-reduce.6
  707.3 98.7 reduce-scatter.3
  813.2 212.4 all-reduce.8
where the time goes:
time: 1100 us; the launch traced here: 1090 us
  waiting for transfers between devices  542 us (49%)
  local copies, waits for them, and re-layouts  213 us (19%)
  matrix products  180 us (16%)
  blocking collectives  64.4 us (6%)
  other arithmetic  48.7 us (4%)
  starting transfers between devices  29.4 us (3%)
  between operations  17.7 us (2%)
    unnamed x6, waiting for transfers between devices  538 us
    dot_general x4, matrix products, attend_backward(): jnp.einsum('hqk,qhd->khd', score_grad, query_block, preferred_element_typ...  50.6 us
    dot_general x4, matrix products, attend_backward(): jnp.einsum('hqk,khd->qhd', score_grad, key_rows, preferred_element_type=j...  49.8 us
    psum x1, blocking collectives, shards(): lax.psum((jnp.sum(grad_shard * grad_shard), gains_local), ('dp', 'sp'))  42.5 us
    unnamed x133, local copies, waits for them, and re-layouts  40.7 us
    convert_element_type x2, local copies, waits for them, and re-layouts, shards(): grad_grid.astype(jnp.bfloat16)  35.1 us
    slice x8, local copies, waits for them, and re-layouts, layer_pieces(): pieces.append(flat_weights[offset:offset + length_now].reshape(dims_pair))  33.5 us
  transfers between devices with their start and end apart: 9, of which 4 were waited for; matrix products, arithmetic and copies ran while one was open for 9% of the time, Pallas kernels for 0%

commit v1 on v0

--- a/solution.py
+++ b/solution.py
@@ -337,7 +337,9 @@
     ).astype(jnp.float32)
     grad_shard = lax.psum_scatter(partial_sum, "dp", scatter_dimension=0, tiled=True).reshape(-1)
     gains_local = jnp.stack([gains_first_grad, gains_second_grad])
-    squares, gains_grad = lax.psum((jnp.sum(grad_shard * grad_shard), gains_local), ("dp", "sp"))
+    squares, gains_grad = lax.psum(
+        lax.psum((jnp.sum(grad_shard * grad_shard), gains_local), "sp"), "dp"
+    )
     grad_norm = jnp.sqrt(squares)
     clipped = grad_shard * jnp.minimum(1.0, 1.0 / grad_norm)
     new_one = 0.5 * moment_one + 0.5 * clipped

time: 1100 us -> 1090 us (level)
  blocking collectives: 64.4 us -> 48.1 us
    psum x1 -> x2, blocking collectives: 42.5 us -> 26.2 us  [the longest x1 19.4 us: shards(): lax.psum(lax.psum((jnp.sum(grad_shard * grad_shard), gains_local), 'sp'),...]
    unnamed x133 -> x131, local copies, waits for them, and re-layouts: 40.7 us -> 40.7 us
where the time goes in v1:
time: 1090 us; the launch traced here: 1080 us
  waiting for transfers between devices  542 us (50%)
  local copies, waits for them, and re-layouts  210 us (19%)
  matrix products  180 us (17%)
  other arithmetic  48.8 us (4%)
  blocking collectives  48.1 us (4%)
  starting transfers between devices  29.4 us (3%)
  between operations  17.7 us (2%)
    unnamed x6, waiting for transfers between devices  538 us
    dot_general x4, matrix products, attend_backward(): jnp.einsum('hqk,qhd->khd', score_grad, query_block, preferred_element_typ...  50.9 us
    dot_general x4, matrix products, attend_backward(): jnp.einsum('hqk,khd->qhd', score_grad, key_rows, preferred_element_type=j...  50.1 us
    unnamed x131, local copies, waits for them, and re-layouts  40.7 us
    convert_element_type x2, local copies, waits for them, and re-layouts, shards(): grad_grid.astype(jnp.bfloat16)  35.1 us
    slice x8, local copies, waits for them, and re-layouts, layer_pieces(): pieces.append(flat_weights[offset:offset + length_now].reshape(dims_pair))  33.1 us
  transfers between devices with their start and end apart: 9, of which 4 were waited for; matrix products, arithmetic and copies ran while one was open for 9% of the time, Pallas kernels for 0%

profile of v1, /device:TPU:12, one launch (start us, length us, event | category | flops | bytes accessed | tf_op | source)
XLA Modules:
  0.0 1076.2 jit_solution(3178908968413588736)
XLA Ops:
  8.4 4.7 broadcast.325
  13.1 7.3 dynamic-update-slice
  22.8 230.3 %all-reduce.8.cloned.1.call-done = bf16[6301696]{0:T(1024)(128)(2,1)} async-done(((bf16[6301696]{0:T(1024)(128)(2,1)}), bf16[6301696]{0:T(1024)(128)(2,1)}) %all-reduce.8.cloned.1.call-update) | async-done | bytes 12603408
  260.8 4.7 all-to-all-start
  281.9 5.8 reshape.1048
  289.2 13.9 %slice.340 = bf16[1368,512]{1,0:T(8,128)(2,1)} reshape(bf16[700416]{0:T(1024)(128)(2,1)} %get-tuple-element.92) | data formatting | bytes 2801664 | tf_op jit(solution)/shard_map/slice | solution.py:33
  333.4 14.3 %all_to_all.108 = bf16[1,256,3,4,128]{1,4,2,0,3:T(8,128)(2,1)S(1)} all-to-all(bf16[1,256,3,4,128]{1,4,2,0,3:T(8,128)(2,1)S(1)} %pad_maximum_fusion.9), channel_id=1, replica_groups=mesh['dp'=8,'sp'=4] {'sp'}, dimensions={3} | all-to-all | bytes 1572864 | tf_op jit(solution)/shard_map/all_to_all | solution.py:173
  371.0 6.1 all-to-all-start.3
  378.5 7.2 reshape.1055
  404.8 7.6 all_to_all.109
  424.6 13.2 %fusion.22 = f32[2,64,1024]{2,1,0:T(8,128)} fusion(f32[2,512,1024]{2,1,0:T(8,128)} %fusion.143, bf16[1024,3,2,64]{0,3,2,1:T(8,128)(2,1)} %squeeze.98, f32[2,512,1024]{2,1,0:T(8,128)} %get-tuple-element.169, f32[2,512]{1,0:T(2,128)S(1)} %log_add_fusion.1, pred[512,1024]{1,0:T(8,128)(4,1)} %get-tuple-element.156), kind=kOutput, calls=%fused_computation.39 | convolution fusion | flops 145754112 | bytes 18489344 | tf_op jit(solution)/shard_map/while/body/eval_jaxpr/hqk,qhd->khd/dot_general | solution.py:147
  437.9 12.8 %fusion.91 = bf16[512,2,64]{0,2,1:T(8,128)(2,1)} fusion(f32[2,512,1024]{2,1,0:T(8,128)} %fusion.143, bf16[1024,3,2,64]{0,3,2,1:T(8,128)(2,1)} %squeeze.98, f32[2,512,1024]{2,1,0:T(8,128)} %get-tuple-element.169, f32[2,512]{1,0:T(2,128)S(1)} %log_add_fusion.1, pred[512,1024]{1,0:T(8,128)(4,1)} %get-tuple-element.156), kind=kOutput, calls=%fused_computation.109 | convolution fusion | flops 145819648 | bytes 18227200 | tf_op jit(solution)/shard_map/while/body/eval_jaxpr/hqk,khd->qhd/dot_general | solution.py:145
  463.1 12.2 %fusion.94 = bf16[512,2,64]{0,2,1:T(8,128)(2,1)} fusion(f32[2,512,1024]{2,1,0:T(8,128)} %fusion.142, bf16[1024,3,2,64]{0,3,2,1:T(8,128)(2,1)} %squeeze.98, f32[2,512,1024]{2,1,0:T(8,128)} %copy-done.30, f32[2,512]{1,0:T(2,128)S(1)} %log_add_fusion, pred[512,1024]{1,0:T(8,128)(4,1)S(1)} %copy-done.21), kind=kOutput, calls=%fused_computation.110 | convolution fusion | flops 145819648 | bytes 18227200 | tf_op jit(solution)/shard_map/while/body/eval_jaxpr/hqk,khd->qhd/dot_general | solution.py:145
  475.4 12.6 %fusion.73 = bf16[2,64,1024]{2,1,0:T(8,128)(2,1)} fusion(f32[2,64,1024]{2,1,0:T(8,128)} %fusion.22, f32[2,512,1024]{2,1,0:T(8,128)} %fusion.142, bf16[1024,3,2,64]{0,3,2,1:T(8,128)(2,1)} %squeeze.98, f32[2,512,1024]{2,1,0:T(8,128)} %copy-done.30, f32[2,512]{1,0:T(2,128)S(1)} %log_add_fusion, pred[512,1024]{1,0:T(8,128)(4,1)S(1)} %copy-done.21), kind=kOutput, calls=%fused_computation.95 | convolution fusion | flops 146016256 | bytes 18751488 | tf_op jit(solution)/shard_map/while/body/eval_jaxpr/hqk,qhd->khd/dot_general | solution.py:147
  497.7 6.3 all-to-all-start.5
  510.1 4.5 copy.134
  514.6 6.4 reshape.1072
  560.9 13.1 %fusion.34 = f32[2,64,1024]{2,1,0:T(8,128)} fusion(f32[2,512,1024]{2,1,0:T(8,128)} %fusion.139, bf16[1024,3,2,64]{0,3,2,1:T(8,128)(2,1)} %copy-done.40, f32[2,512,1024]{2,1,0:T(8,128)} %copy-done.29, f32[2,512]{1,0:T(2,128)S(1)} %log_add_fusion.3, pred[512,1024]{1,0:T(8,128)(4,1)} %get-tuple-element.156), kind=kOutput, calls=%fused_computation.43 | convolution fusion | flops 145754112 | bytes 18489344 | tf_op jit(solution)/shard_map/while/body/eval_jaxpr/hqk,qhd->khd/dot_general | solution.py:147
  574.0 12.8 %fusion.97 = bf16[512,2,64]{0,2,1:T(8,128)(2,1)} fusion(f32[2,512,1024]{2,1,0:T(8,128)} %fusion.139, bf16[1024,3,2,64]{0,3,2,1:T(8,128)(2,1)} %copy-done.40, f32[2,512,1024]{2,1,0:T(8,128)} %copy-done.29, f32[2,512]{1,0:T(2,128)S(1)} %log_add_fusion.3, pred[512,1024]{1,0:T(8,128)(4,1)} %get-tuple-element.156), kind=kOutput, calls=%fused_computation.111 | convolution fusion | flops 145819648 | bytes 18227200 | tf_op jit(solution)/shard_map/while/body/eval_jaxpr/hqk,khd->qhd/dot_general | solution.py:145
  592.8 12.3 %fusion.100 = bf16[512,2,64]{0,2,1:T(8,128)(2,1)} fusion(f32[2,512,1024]{2,1,0:T(8,128)} %fusion.138, bf16[1024,3,2,64]{0,3,2,1:T(8,128)(2,1)} %copy-done.40, f32[2,512,1024]{2,1,0:T(8,128)} %copy-done.27, f32[2,512]{1,0:T(2,128)S(1)} %log_add_fusion.2, pred[512,1024]{1,0:T(8,128)(4,1)S(1)} %copy-done.21), kind=kOutput, calls=%fused_computation.112 | convolution fusion | flops 145819648 | bytes 18227200 | tf_op jit(solution)/shard_map/while/body/eval_jaxpr/hqk,khd->qhd/dot_general | solution.py:145
  605.1 12.0 %fusion.76 = bf16[2,64,1024]{2,1,0:T(8,128)(2,1)S(1)} fusion(f32[2,64,1024]{2,1,0:T(8,128)} %fusion.34, f32[2,512,1024]{2,1,0:T(8,128)} %fusion.138, bf16[1024,3,2,64]{0,3,2,1:T(8,128)(2,1)} %copy-done.40, f32[2,512,1024]{2,1,0:T(8,128)} %copy-done.27, f32[2,512]{1,0:T(2,128)S(1)} %log_add_fusion.2, pred[512,1024]{1,0:T(8,128)(4,1)S(1)} %copy-done.21), kind=kOutput, calls=%fused_computation.96 | convolution fusion | flops 146016256 | bytes 18751488 | tf_op jit(solution)/shard_map/while/body/eval_jaxpr/hqk,qhd->khd/dot_general | solution.py:147
  623.4 4.6 all-to-all-start.7
  629.3 4.9 copy.133
  634.3 6.5 reshape.1067
  669.9 23.6 %convert_element_type.303 = bf16[8,4,196928]{2,1,0:T(4,128)(2,1)} reshape(bf16[6301696]{0:T(1024)(128)(2,1)} %constant_dynamic-update-slice_fusion) | data formatting | bytes 25206784 | tf_op jit(solution)/shard_map/convert_element_type | solution.py:336
  693.5 11.5 %copy.135 = bf16[8,4,196928]{2,0,1:T(8,128)(2,1)} copy(bf16[8,4,196928]{2,1,0:T(4,128)(2,1)} %convert_element_type.303) | data formatting | bytes 25206784 | tf_op jit(solution)/shard_map/convert_element_type | solution.py:336
  705.1 98.9 %reduce-scatter.4.cloned.1.call-done = bf16[8,1,196928]{2,0,1:T(8,128)(2,1)} async-done(((bf16[8,4,196928]{2,0,1:T(8,128)(2,1)}), bf16[8,1,196928]{2,0,1:T(8,128)(2,1)}) %reduce-scatter.4.cloned.1.call-update) | async-done | bytes 3150864
  804.0 6.9 copy.136
  815.1 208.4 %all-reduce.10.cloned.1.call-done = f32[8,1,196928]{2,1,0:T(1,128)} async-done(((f32[8,1,196928]{2,1,0:T(1,128)}), f32[8,1,196928]{2,1,0:T(1,128)}) %all-reduce.10.cloned.1.call-update) | async-done | bytes 6301712
  1028.9 6.8 all-reduce.4
  1035.6 19.4 %all-reduce.3 = (f32[]{:T(128)}, f32[2,2,512]{2,1,0:T(2,128)}) all-reduce(f32[]{:T(128)} %get-tuple-element.78, f32[2,2,512]{2,1,0:T(2,128)S(1)} %get-tuple-element.79), channel_id=1, replica_groups=mesh['dp'=8,'sp'=4] {'dp'}, use_global_device_ids=true, to_apply=%region_28.29 | all-reduce | flops 2049 | bytes 16392 | tf_op jit(solution)/shard_map/psum | solution.py:340
  1055.8 9.0 multiply_reduce_fusion.4
  (308 shorter events, 237.6 us)
Async XLA Ops:
  7.2 245.9 %all-reduce.8.cloned.1.call-start = ((), (), s32[]{:S(2)}) async-start(), calls=%async_computation.9 | async-start | bytes 25206784
  260.8 43.0 %all-to-all-start = ((bf16[1,256,3,4,128]{1,4,2,0,3:T(8,128)(2,1)}), bf16[1,256,3,4,128]{1,4,2,0,3:T(8,128)(2,1)}, u32[]{:S(2)}, u32[]{:S(2)}) async-start(bf16[1,256,3,4,128]{1,4,2,0,3:T(8,128)(2,1)} %pad_maximum_fusion.8), calls=%async_computation | async-start | bytes 1572864 | tf_op jit(solution)/shard_map/all_to_all | solution.py:173
  287.7 18.4 %copy-start.21 = (pred[512,1024]{1,0:T(8,128)(4,1)S(1)}, pred[512,1024]{1,0:T(8,128)(4,1)}, u32[]{:S(2)}) copy-start(pred[512,1024]{1,0:T(8,128)(4,1)} %get-tuple-element.157) | copy-start | bytes 1572868
  289.1 37.0 %copy-start.25 = (bf16[512,512]{1,0:T(8,128)(2,1)}, bf16[512,512]{1,0:T(8,128)(2,1)S(1)}, u32[]{:S(2)}) copy-start(bf16[512,512]{1,0:T(8,128)(2,1)S(1)} %slice.333) | copy-start | bytes 1572868
  306.1 6.1 copy-start.40
  313.5 12.7 %copy-start.38 = (bf16[1,256,512]{2,1,0:T(8,128)(2,1)S(1)}, bf16[1,256,512]{2,1,0:T(8,128)(2,1)}, u32[]{:S(2)}) copy-start(bf16[1,256,512]{2,1,0:T(8,128)(2,1)} %param.6) | copy-start | bytes 786436
  317.9 7.8 all-to-all-start.1
  326.1 4.2 copy-start.35
  353.9 4.5 copy-start.30
  371.0 18.2 %all-to-all-start.3 = ((bf16[4,2,16384]{2,1,0:T(2,128)(2,1)}), bf16[4,2,16384]{2,1,0:T(2,128)(2,1)}, u32[]{:S(2)}, u32[]{:S(2)}) async-start(bf16[4,2,16384]{2,1,0:T(2,128)(2,1)} %reshape.1086), calls=%async_computation.3 | async-start | bytes 524288 | tf_op jit(solution)/shard_map/all_to_all | solution.py:179
  378.5 14.5 %copy-start.23 = (bf16[512,512]{1,0:T(8,128)(2,1)}, bf16[512,512]{1,0:T(8,128)(2,1)S(1)}, u32[]{:S(2)}) copy-start(bf16[512,512]{1,0:T(8,128)(2,1)S(1)} %slice.359) | copy-start | bytes 1572868
  392.9 4.7 copy-start.15
  392.9 4.7 copy-start.42
  416.4 4.5 copy-start.51
  454.0 3.9 copy-start.31
  454.0 3.9 copy-start.50
  497.7 27.0 %all-to-all-start.5 = ((bf16[1,1024,3,1,128]{4,2,3,0,1:T(4,128)(2,1)}), bf16[1,1024,3,1,128]{4,2,3,0,1:T(4,128)(2,1)}, u32[]{:S(2)}, u32[]{:S(2)}) async-start(bf16[1,1024,3,1,128]{4,2,3,0,1:T(4,128)(2,1)} %pad_maximum_fusion.2), calls=%async_computation.5 | async-start | bytes 2097152 | tf_op jit(solution)/shard_map/all_to_all | solution.py:203
  538.1 89.9 %copy-start.8 = (f32[1,256,512]{2,1,0:T(8,128)}, f32[1,256,512]{2,1,0:T(8,128)S(1)}, u32[]{:S(2)}) copy-start(f32[1,256,512]{2,1,0:T(8,128)S(1)} %multiply_subtract_fusion) | copy-start | bytes 1572868
  542.6 9.7 all-to-all-start.6
  546.8 3.9 copy-start.45
  617.1 11.0 %copy-start.36 = (bf16[1,256,4,1,128]{1,4,2,3,0:T(8,128)(2,1)S(1)}, bf16[1,256,4,1,128]{1,4,2,3,0:T(8,128)(2,1)}, u32[]{:S(2)}) copy-start(bf16[1,256,4,1,128]{1,4,2,3,0:T(8,128)(2,1)} %copy-done.35) | copy-start | bytes 786436
  623.4 23.1 %all-to-all-start.7 = ((bf16[1,1024,3,1,128]{4,2,3,0,1:T(4,128)(2,1)}), bf16[1,1024,3,1,128]{4,2,3,0,1:T(4,128)(2,1)}, u32[]{:S(2)}, u32[]{:S(2)}) async-start(bf16[1,1024,3,1,128]{4,2,3,0,1:T(4,128)(2,1)} %pad_maximum_fusion.3), calls=%async_computation.7 | async-start | bytes 2097152 | tf_op jit(solution)/shard_map/all_to_all | solution.py:203
  628.0 176.0 %reduce-scatter.4.cloned.1.call-start = ((), (), s32[]{:S(2)}) async-start(), calls=%async_computation.11 | async-start | bytes 15759360
  634.3 6.6 copy-start.16
  634.3 8.4 copy-start.34
  651.8 9.1 copy-start.7
  656.2 6.4 copy-start.20
  662.6 3.9 copy-start.6
  705.0 318.5 %all-reduce.10.cloned.1.call-start = ((), (), s32[]{:S(2)}) async-start(), calls=%async_computation.10 | async-start | bytes 12607488
  810.9 216.6 %copy-start.1 = (bf16[512,1536]{1,0:T(8,128)(2,1)S(1)}, bf16[512,1536]{1,0:T(8,128)(2,1)}, u32[]{:S(2)}) copy-start(bf16[512,1536]{1,0:T(8,128)(2,1)} %copy-done) | copy-start | bytes 4718596
  810.9 216.6 %copy-start.9 = (f32[1,256,512]{2,1,0:T(8,128)S(1)}, f32[1,256,512]{2,1,0:T(8,128)}, u32[]{:S(2)}) copy-start(f32[1,256,512]{2,1,0:T(8,128)} %copy-done.8) | copy-start | bytes 1572868
  810.9 216.6 %copy-start.11 = (bf16[1,256,3,8,64]{1,4,3,2,0:T(8,128)(2,1)S(1)}, bf16[1,256,3,8,64]{1,4,3,2,0:T(8,128)(2,1)}, u32[]{:S(2)}) copy-start(bf16[1,256,3,8,64]{1,4,3,2,0:T(8,128)(2,1)} %copy-done.10) | copy-start | bytes 2359300
  (30 other events, 66.4 us)
Sparse Core Ops, SparseCore 0:
  20.5 232.5 all-reduce.7
  705.1 98.7 reduce-scatter.3
  811.1 212.4 all-reduce.9
